TPU v7x, 32 devices: a whole 2x2x4 slice. The times are simulated.
32 devices in a mesh: groups: 2 (over x), long: 16 (over z, y, core).
Axes of the slice: x: 2, y: 2, z: 4, core: 2. Of those that a mesh axis runs over, the one named last changes fastest.
Arguments:
- displacement: float32 [4, 2, 128, 16, 256], P('groups', None, 'long'), parts along dimension 0, may hold values from -6 to 6
- velocity: float32 [4, 2, 128, 16, 256], P('groups', None, 'long'), parts along dimension 0, may hold values from -4 to 4
- damage: float32 [4, 128, 16, 256], P('groups', 'long'), parts along dimension 0, may hold values from 0 to 0.6
- material: int32 [4, 128, 16, 256], P('groups', 'long'), parts along dimension 0, may hold values from 0 to 3
- damage_table: float32 [2, 4], replicated, may hold values from 0.1 to 2
- fault_rows: int32 [4, 128, 16], P('groups', 'long'), parts along dimension 0, may hold values from 0 to 3
- kernel: float32 [16, 64, 2, 2], P(None, 'long'), may hold values from -1.5 to 1.5
- history: float32 [30, 64, 2, 2, 16], P('groups', 'long'), parts along dimension 0, may hold values from -6 to 6
Outputs:
- displacement_out: float32 [4, 2, 128, 16, 256], P('groups', None, 'long'), parts along dimension 0
- velocity_out: float32 [4, 2, 128, 16, 256], P('groups', None, 'long'), parts along dimension 0
- damage_out: float32 [4, 128, 16, 256], P('groups', 'long'), parts along dimension 0
- history_out: float32 [30, 64, 2, 2, 16], P('groups', 'long'), parts along dimension 0
There are 2 independent parts, one for each index of `groups`. A program takes and returns all parts, laid end to end along the dimension named above; an argument that names none is the same for every part. Nothing has to cross between parts.
Inputs may be any that keep to these rules, and one draw needn't show every extreme that they name: `fault_rows`: row of the fault face, counted from the fault.
All inputs are finite; a program needn't handle non-finite values.
Results may differ from a plain program's by a relative error of at most 0.00011.
Values sent between devices are 32-bit elements; how exact they have to be, the bound alone decides.
A program may use at most 64 MiB of HBM per device.

v0:
```python
import math
import jax
import jax.numpy as jnp
from jax import lax
from jax.sharding import PartitionSpec as P

STEPS = 2
time_step = 0.5


def padded_2(block, sides, width):
    for axis, dim in sides:
        count = lax.axis_size(axis)
        forward = [(i, i + 1) for i in range(count - 1)]
        forward.append((count - 1, 0))
        backward = [(target, source) for source, target in forward]
        low = lax.ppermute(
            lax.slice_in_dim(block, block.shape[dim] - width, None, axis=dim), axis, forward
        )
        high = lax.ppermute(lax.slice_in_dim(block, 0, width, axis=dim), axis, backward)
        block = jnp.concatenate([low, block, high], axis=dim)
    return block


def class_lookup(material, table_row):
    result = jnp.zeros(material.shape, table_row.dtype)
    for level in range(table_row.shape[0]):
        result = result + jnp.where(
            material == level, table_row[level], jnp.zeros((), table_row.dtype)
        )
    return result


def neighbour(values_in, axis, higher):
    selector = [slice(None)] * values_in.ndim
    for dimension in range(values_in.ndim - 3, values_in.ndim):
        selector[dimension] = slice(1, -1)
    selector[axis] = slice(2, None) if higher else slice(0, -2)
    return values_in[tuple(selector)]


def local_terms(padded_u, padded_c):
    outer_u = jnp.pad(padded_u, ((0, 0), (0, 0), (0, 0), (1, 1), (1, 1)))
    outer_c = jnp.pad(padded_c, ((0, 0), (0, 0), (1, 1), (1, 1)), mode="edge")
    centre_u = outer_u[:, :, 1:-1, 1:-1, 1:-1]
    centre_c = outer_c[:, 1:-1, 1:-1, 1:-1]
    forces = jnp.zeros_like(centre_u)
    energy = jnp.zeros_like(centre_c)
    for offset in range(3):
        above_u = neighbour(outer_u, 2 + offset, True)
        below_u = neighbour(outer_u, 2 + offset, False)
        above_c = neighbour(outer_c, 1 + offset, True)
        below_c = neighbour(outer_c, 1 + offset, False)
        forces = forces + (0.5 * (centre_c + above_c))[None] * (above_u - centre_u)
        forces = forces + (0.5 * (centre_c + below_c))[None] * (below_u - centre_u)
        gradient = 0.5 * (above_u - below_u)
        energy = energy + jnp.sum(gradient * gradient, axis=0)
    return (forces, energy)


def convolve(kernel, stacked):
    kernel_real = kernel[:, :, 0, :, None]
    kernel_imag = kernel[:, :, 1, :, None]
    spec_real = stacked[:, :, 0]
    spec_imag = stacked[:, :, 1]
    out_real = jnp.sum(kernel_real * spec_real - kernel_imag * spec_imag, axis=0)
    out_imag = jnp.sum(kernel_real * spec_imag + kernel_imag * spec_real, axis=0)
    return (out_real, out_imag)


def basis(waves, places, length):
    phase = (waves[:, None] * places[None, :] % length).astype(jnp.float32) * (
        2.0 * math.pi / length
    )
    return (jnp.cos(phase), jnp.sin(phase))


def spectral_terms(cosine, sine_table, slip_part, norming):
    part_real = (
        jnp.einsum("kx,cxz->kcz", cosine, slip_part, precision=lax.Precision.HIGHEST) * norming
    )
    part_imag = (
        -jnp.einsum("kx,cxz->kcz", sine_table, slip_part, precision=lax.Precision.HIGHEST) * norming
    )
    return jnp.stack([part_real, part_imag], 1)


def wave_sum(waves, places, spectrum, length, norming):
    cosine, sine_table = basis(waves, places, length)
    weights = jnp.where(waves == 0, 1.0, 2.0).astype(jnp.float32) * norming
    first_part = jnp.einsum(
        "kx,kcz->cxz", cosine * weights[:, None], spectrum[:, 0], precision=lax.Precision.HIGHEST
    )
    second_part = jnp.einsum(
        "kx,kcz->cxz",
        sine_table * weights[:, None],
        spectrum[:, 1],
        precision=lax.Precision.HIGHEST,
    )
    return first_part - second_part


def advance(
    disp_mid, vel_mid, dmg_mid, rate_mid, limit_mid, fault_mid, forces, energy, traction, signs
):
    pushes = traction[:, None, :, :, None] * signs[None] * fault_mid[None]
    vel_new = vel_mid + time_step * (forces + pushes)
    disp_new = disp_mid + time_step * vel_new
    dmg_new = 1.0 - (1.0 - dmg_mid) * jnp.exp(-rate_mid * jax.nn.softplus(energy - limit_mid))
    return (disp_new, vel_new, dmg_new)


def per_device(displacement, velocity, damage, material, damage_table, fault_rows, kernel, history):
    cells = displacement.shape[2]
    position = lax.axis_index("long")
    length = cells * lax.axis_size("long")
    owned = cells // 2
    norming = 1.0 / math.sqrt(length)
    rates = class_lookup(material, damage_table[0])
    limits = class_lookup(material, damage_table[1])
    heights = lax.broadcasted_iota(jnp.int32, damage.shape, 3)
    on_fault = (heights == fault_rows[..., None]).astype(displacement.dtype)
    signs = jnp.array([1.0, -1.0], displacement.dtype)[:, None, None, None]
    lagged = [history[level] for level in range(history.shape[0])]
    for number in range(STEPS):
        stiffness = 1.0 - damage
        stacked_fields = jnp.concatenate([displacement, stiffness[None]], 0)
        padded = padded_2(stacked_fields, (("long", 2),), 1)
        forces, energy = local_terms(padded[:-1], padded[-1])
        own_disp = displacement
        face = jnp.sum(own_disp * on_fault[None], axis=4)
        slip = face[:, 1] - face[:, 0]
        waves = jnp.arange(lax.axis_size("long") * owned, dtype=jnp.int32)
        places = position * cells + jnp.arange(cells, dtype=jnp.int32)
        cosine, sine_table = basis(waves, places, length)
        current = lax.psum_scatter(
            spectral_terms(cosine, sine_table, slip, norming),
            "long",
            scatter_dimension=0,
            tiled=True,
        )
        stacked_lags = jnp.stack([current] + lagged, 0)
        traction_real, traction_imag = convolve(kernel, stacked_lags)
        traction_spectrum = jnp.stack([traction_real, traction_imag], 1)

        def add_waves(piece):
            waves = jnp.arange(piece.shape[0], dtype=jnp.int32)
            places = position * cells + jnp.arange(cells, dtype=jnp.int32)
            return wave_sum(waves, places, piece, length, norming)

        traction = add_waves(lax.all_gather(traction_spectrum, "long", axis=0, tiled=True))
        displacement, velocity, damage = advance(
            displacement, velocity, damage, rates, limits, on_fault, forces, energy, traction, signs
        )
        lagged = [current] + lagged[:-1]
    return (displacement, velocity, damage, jnp.stack(lagged, 0))


def solution(mesh):
    placed = (
        P("groups", None, "long", None, None),
        P("groups", None, "long", None, None),
        P("groups", "long", None, None),
        P("groups", "long", None, None),
        P(),
        P("groups", "long", None),
        P(None, "long", None, None),
        P("groups", "long", None, None, None),
    )
    return jax.shard_map(
        per_device,
        mesh=mesh,
        in_specs=placed,
        out_specs=(
            P("groups", None, "long", None, None),
            P("groups", None, "long", None, None),
            P("groups", "long", None, None),
            P("groups", "long", None, None, None),
        ),
        check_vma=False,
    )
```

profile of v0, /device:TPU:0, one launch (start us, length us, event | category | flops | bytes accessed | tf_op | source)
XLA Modules:
  0.0 214.8 jit_solution(16481410820871778354)
XLA Ops:
  0.7 1.0 subtract_bitcast_fusion
  1.7 0.9 pad_maximum_fusion.31
  3.1 5.1 %collective-permute-start.1 = (f32[3,2,1,16,256]{4,3,2,1,0:T(8,128)S(1)}, f32[3,2,1,16,256]{4,3,2,1,0:T(8,128)S(1)}, u32[]{:S(2)}, u32[]{:S(2)}) collective-permute-start(f32[3,2,1,16,256]{4,3,2,1,0:T(8,128)S(1)} %get-tuple-element.28), channel_id=1, source_target_pairs={{1,0},{2,1},{3,2},{4,3},{5,4},{6,5},{7,6},{8,7},{9,8},{10,9},{11,1... | collective-permute-start | bytes 294920 | tf_op jit(solution)/shard_map/ppermute | solution.py:20
  8.8 0.7 fusion.127
  9.8 0.6 dynamic-slice
  11.5 1.4 multiply_reduce_fusion.5
  13.5 0.7 fusion.38
  14.3 0.9 fusion.122
  15.3 62.3 %all-reduce.2 = f32[64,2,2,16]{3,2,1,0:T(2,128)S(1)} all-reduce(f32[64,2,2,16]{3,2,1,0:T(2,128)S(1)} %copy.50), channel_id=2, replica_groups=mesh['groups'=2,'long'=16] {'long'}, use_global_device_ids=true, to_apply=%region_1.2.clone | all-reduce | flops 4096 | bytes 32768
  77.9 17.5 %all_gather.6 = f32[64,2,2,16]{3,2,1,0:T(2,128)S(1)} all-gather(f32[4,2,2,16]{3,2,1,0:T(2,128)S(1)} %copy.54), channel_id=1, replica_groups=mesh['groups'=2,'long'=16] {'long'}, dimensions={0}, use_global_device_ids=true | all-gather | bytes 17408 | tf_op jit(solution)/shard_map/all_gather | solution.py:151
  95.6 1.5 fusion.33
  97.8 6.1 %fusion.15 = (f32[2,8,16,256]{3,2,1,0:T(8,128)S(1)}, pred[2,8,16,256]{3,2,1,0:T(8,128)(4,1)}, pred[2,8,16,256]{3,2,1,0:T(8,128)(4,1)}, pred[2,8,16,256]{3,2,1,0:T(8,128)(4,1)}, pred[2,8,16,256]{3,2,1,0:T(8,128)(4,1)}) fusion(f32[2,8,16,256]{3,2,1,0:T(8,128)S(1)} %copy-done.5, f32[2,8,16,256]{3,2,1,0:T(8,128)S(1)} %copy-done.6, ...), kind=kLoop, calls=%fused_computation.57 | loop fusion | flops 2162688 | bytes 1835040 | tf_op jit(solution)/shard_map/sub | solution.py:126
  104.0 1.5 multiply_add_fusion.2
  105.9 4.1 %collective-permute-start.3 = (f32[3,2,1,16,256]{4,3,2,1,0:T(8,128)S(1)}, f32[3,2,1,16,256]{4,3,2,1,0:T(8,128)S(1)}, u32[]{:S(2)}, u32[]{:S(2)}) collective-permute-start(f32[3,2,1,16,256]{4,3,2,1,0:T(8,128)S(1)} %get-tuple-element.26), channel_id=1, source_target_pairs={{1,0},{2,1},{3,2},{4,3},{5,4},{6,5},{7,6},{8,7},{9,8},{10,9},{11,1... | collective-permute-start | bytes 294920 | tf_op jit(solution)/shard_map/ppermute | solution.py:20
  110.0 0.6 slice.347
  110.7 1.8 collective-permute-done.2
  112.5 0.7 fusion.28
  113.2 0.9 multiply_reduce_fusion.2
  115.1 1.3 multiply_reduce_fusion.1
  116.5 0.8 fusion.121
  117.2 0.8 copy.57
  118.0 63.8 %all-reduce.3 = f32[64,2,2,16]{3,2,1,0:T(2,128)} all-reduce(f32[64,2,2,16]{3,2,1,0:T(2,128)} %copy.57), channel_id=3, replica_groups=mesh['groups'=2,'long'=16] {'long'}, use_global_device_ids=true, to_apply=%region_8.9.clone | all-reduce | flops 4096 | bytes 32768
  181.8 0.7 dynamic-slice_bitcast_fusion
  182.8 17.5 %all_gather.7 = f32[64,2,2,16]{3,2,1,0:T(2,128)S(1)} all-gather(f32[4,2,2,16]{3,2,1,0:T(2,128)S(1)} %copy.61), channel_id=1, replica_groups=mesh['groups'=2,'long'=16] {'long'}, dimensions={0}, use_global_device_ids=true | all-gather | bytes 17408 | tf_op jit(solution)/shard_map/all_gather | solution.py:151
  200.3 0.7 fusion.125
  200.9 0.9 copy.72
  201.8 0.9 fusion.45
  202.9 0.9 fusion.9
  203.9 1.7 pad_maximum_fusion.27
  205.6 1.3 fusion.23
  207.0 6.2 %fusion.19 = f32[2,8,16,256]{3,2,1,0:T(8,128)} fusion(f32[2,8,16,256]{3,2,1,0:T(8,128)S(1)} %get-tuple-element.18, f32[2,8,16,256]{3,2,1,0:T(8,128)S(1)} %copy-done.9, f32[2,8,16,256]{3,2,1,0:T(8,128)S(1)} %copy-done.10, f32[2,8,16,256]{3,2,1,0:T(8,128)S(1)} %copy-done.8, pred[2,8,16,256]{3,2,1,0:T(8,128)(4,1)S(1)} %copy-done.20, ...), kind=kLoop, calls=%fused_computation.61 | loop fusion | flops 1769472 | bytes 1572896 | tf_op jit(solution)/shard_map/sub | solution.py:109
  213.2 1.6 multiply_add_fusion
  (103 shorter events, 6.0 us)
Async XLA Ops:
  0.6 9.1 %copy-start.27 = (u32[32]{0:T(128)S(1)}, u32[32]{0:T(128)}, u32[]{:S(2)}) copy-start(u32[32]{0:T(128)} %constant.74) | copy-start | bytes 388
  0.6 10.4 %copy-start = (f32[2,2,8,16,256]{4,3,2,1,0:T(8,128)S(1)}, f32[2,2,8,16,256]{4,3,2,1,0:T(8,128)}, u32[]{:S(2)}) copy-start(f32[2,2,8,16,256]{4,3,2,1,0:T(8,128)} %param.9) | copy-start | bytes 1572868
  0.7 8.1 %copy-start.24 = (s32[2,8,16]{2,1,0:T(8,128)S(1)}, s32[2,8,16]{2,1,0:T(8,128)}, u32[]{:S(2)}) copy-start(s32[2,8,16]{2,1,0:T(8,128)} %param.14) | copy-start | bytes 3076
  0.7 8.2 %copy-start.23 = (f32[2,4]{1,0:T(2,128)S(1)}, f32[2,4]{1,0:T(2,128)}, u32[]{:S(2)}) copy-start(f32[2,4]{1,0:T(2,128)} %param.13) | copy-start | bytes 100
  0.7 8.8 %copy-start.25 = (f32[16,4,2,2]{0,3,2,1:T(2,128)S(1)}, f32[16,4,2,2]{0,3,2,1:T(2,128)}, u32[]{:S(2)}) copy-start(f32[16,4,2,2]{0,3,2,1:T(2,128)} %param.15) | copy-start | bytes 3076
  2.6 8.4 %collective-permute-start = (f32[3,2,1,16,256]{4,3,2,1,0:T(8,128)S(1)}, f32[3,2,1,16,256]{4,3,2,1,0:T(8,128)S(1)}, u32[]{:S(2)}, u32[]{:S(2)}) collective-permute-start(f32[3,2,1,16,256]{4,3,2,1,0:T(8,128)S(1)} %get-tuple-element.27), channel_id=1, source_target_pairs={{0,1},{1,2},{2,3},{3,4},{4,5},{5,6},{6,7},{7,8},{8,9},{9,10},{10,1... | collective-permute-start | bytes 294920 | tf_op jit(solution)/shard_map/ppermute | solution.py:17
  3.1 7.9 %collective-permute-start.1 = (f32[3,2,1,16,256]{4,3,2,1,0:T(8,128)S(1)}, f32[3,2,1,16,256]{4,3,2,1,0:T(8,128)S(1)}, u32[]{:S(2)}, u32[]{:S(2)}) collective-permute-start(f32[3,2,1,16,256]{4,3,2,1,0:T(8,128)S(1)} %get-tuple-element.28), channel_id=1, source_target_pairs={{1,0},{2,1},{3,2},{4,3},{5,4},{6,5},{7,6},{8,7},{9,8},{10,9},{11,1... | collective-permute-start | bytes 294920 | tf_op jit(solution)/shard_map/ppermute | solution.py:20
  9.7 67.9 %copy-start.14 = (f32[16,4,2]{2,1,0:T(4,128)}, f32[16,4,2]{2,1,0:T(4,128)S(1)}, u32[]{:S(2)}) copy-start(f32[16,4,2]{2,1,0:T(4,128)S(1)} %copy.53) | copy-start | bytes 1540
  13.5 64.1 %copy-start.11 = (f32[15,4,2,2,16]{4,3,2,1,0:T(2,128)S(1)}, f32[15,4,2,2,16]{4,3,2,1,0:T(2,128)}, u32[]{:S(2)}) copy-start(f32[15,4,2,2,16]{4,3,2,1,0:T(2,128)} %param.16) | copy-start | bytes 46084
  95.4 2.3 %copy-start.26 = (f32[2]{0:T(128)S(1)}, f32[2]{0:T(128)}, u32[]{:S(2)}) copy-start(f32[2]{0:T(128)} %constant.60.clone) | copy-start | bytes 28
  95.6 2.2 %copy-start.4 = (f32[2,8,16,256]{3,2,1,0:T(8,128)S(1)}, f32[2,8,16,256]{3,2,1,0:T(8,128)}, u32[]{:S(2)}) copy-start(f32[2,8,16,256]{3,2,1,0:T(8,128)} %get-tuple-element.6) | copy-start | bytes 786436
  95.6 2.2 %copy-start.5 = (f32[2,8,16,256]{3,2,1,0:T(8,128)S(1)}, f32[2,8,16,256]{3,2,1,0:T(8,128)}, u32[]{:S(2)}) copy-start(f32[2,8,16,256]{3,2,1,0:T(8,128)} %get-tuple-element.7) | copy-start | bytes 786436
  95.6 2.2 %copy-start.6 = (f32[2,8,16,256]{3,2,1,0:T(8,128)S(1)}, f32[2,8,16,256]{3,2,1,0:T(8,128)}, u32[]{:S(2)}) copy-start(f32[2,8,16,256]{3,2,1,0:T(8,128)} %get-tuple-element.62) | copy-start | bytes 786436
  95.6 2.2 %copy-start.7 = (f32[2,8,16,256]{3,2,1,0:T(8,128)S(1)}, f32[2,8,16,256]{3,2,1,0:T(8,128)}, u32[]{:S(2)}) copy-start(f32[2,8,16,256]{3,2,1,0:T(8,128)} %param.11) | copy-start | bytes 786436
  97.1 6.9 %copy-start.3 = (f32[2,8,16,256]{3,2,1,0:T(8,128)S(1)}, f32[2,8,16,256]{3,2,1,0:T(8,128)}, u32[]{:S(2)}) copy-start(f32[2,8,16,256]{3,2,1,0:T(8,128)} %fusion.38) | copy-start | bytes 786436
  97.1 6.9 %copy-start.13 = (f32[2,2,8,16,256]{4,3,2,1,0:T(8,128)S(1)}, f32[2,2,8,16,256]{4,3,2,1,0:T(8,128)}, u32[]{:S(2)}) copy-start(f32[2,2,8,16,256]{4,3,2,1,0:T(8,128)} %param.10) | copy-start | bytes 1572868
  104.0 6.0 %copy-start.12 = (f32[15,4,2,2,16]{4,3,2,1,0:T(2,128)S(1)}, f32[15,4,2,2,16]{4,3,2,1,0:T(2,128)}, u32[]{:S(2)}) copy-start(f32[15,4,2,2,16]{4,3,2,1,0:T(2,128)} %param.16) | copy-start | bytes 46084
  105.5 6.9 %collective-permute-start.2 = (f32[3,2,1,16,256]{4,3,2,1,0:T(8,128)S(1)}, f32[3,2,1,16,256]{4,3,2,1,0:T(8,128)S(1)}, u32[]{:S(2)}, u32[]{:S(2)}) collective-permute-start(f32[3,2,1,16,256]{4,3,2,1,0:T(8,128)S(1)} %get-tuple-element.25), channel_id=1, source_target_pairs={{0,1},{1,2},{2,3},{3,4},{4,5},{5,6},{6,7},{7,8},{8,9},{9,10},{10,1... | collective-permute-start | bytes 294920 | tf_op jit(solution)/shard_map/ppermute | solution.py:17
  105.9 6.5 %collective-permute-start.3 = (f32[3,2,1,16,256]{4,3,2,1,0:T(8,128)S(1)}, f32[3,2,1,16,256]{4,3,2,1,0:T(8,128)S(1)}, u32[]{:S(2)}, u32[]{:S(2)}) collective-permute-start(f32[3,2,1,16,256]{4,3,2,1,0:T(8,128)S(1)} %get-tuple-element.26), channel_id=1, source_target_pairs={{1,0},{2,1},{3,2},{4,3},{5,4},{6,5},{7,6},{8,7},{9,8},{10,9},{11,1... | collective-permute-start | bytes 294920 | tf_op jit(solution)/shard_map/ppermute | solution.py:20
  112.5 3.9 %copy-start.21 = (f32[2,10,1,256]{3,2,1,0:T(1,128)}, f32[2,10,1,256]{3,2,1,0:T(1,128)S(1)}, u32[]{:S(2)}) copy-start(f32[2,10,1,256]{3,2,1,0:T(1,128)S(1)} %get-tuple-element.43) | copy-start | bytes 61444
  112.5 3.9 %copy-start.22 = (f32[2,10,1,256]{3,2,1,0:T(1,128)}, f32[2,10,1,256]{3,2,1,0:T(1,128)S(1)}, u32[]{:S(2)}) copy-start(f32[2,10,1,256]{3,2,1,0:T(1,128)S(1)} %get-tuple-element.44) | copy-start | bytes 61444
  116.4 66.1 %slice-start = ((f32[15,4,2,2,16]{4,3,2,1,0:T(2,128)}), f32[14,4,2,2,16]{4,3,2,1,0:T(2,128)S(1)}, s32[]{:S(2)}) async-start(f32[15,4,2,2,16]{4,3,2,1,0:T(2,128)} %param.16), calls=%async_computation | async-start | bytes 229376 | tf_op jit(solution)/shard_map/slice | solution.py:124
  116.4 66.2 %copy-start.15 = (f32[16,4,2]{2,1,0:T(4,128)S(1)}, f32[16,4,2]{2,1,0:T(4,128)}, u32[]{:S(2)}) copy-start(f32[16,4,2]{2,1,0:T(4,128)} %copy-done.14) | copy-start | bytes 1540
  203.9 3.1 %copy-start.8 = (f32[2,8,16,256]{3,2,1,0:T(8,128)S(1)}, f32[2,8,16,256]{3,2,1,0:T(8,128)}, u32[]{:S(2)}) copy-start(f32[2,8,16,256]{3,2,1,0:T(8,128)} %get-tuple-element.4) | copy-start | bytes 786436
  203.9 3.1 %copy-start.9 = (f32[2,8,16,256]{3,2,1,0:T(8,128)S(1)}, f32[2,8,16,256]{3,2,1,0:T(8,128)}, u32[]{:S(2)}) copy-start(f32[2,8,16,256]{3,2,1,0:T(8,128)} %get-tuple-element.5) | copy-start | bytes 786436
  203.9 3.1 %copy-start.10 = (f32[2,8,16,256]{3,2,1,0:T(8,128)S(1)}, f32[2,8,16,256]{3,2,1,0:T(8,128)}, u32[]{:S(2)}) copy-start(f32[2,8,16,256]{3,2,1,0:T(8,128)} %get-tuple-element.8) | copy-start | bytes 786436
  203.9 3.1 %copy-start.17 = (pred[2,8,16,256]{3,2,1,0:T(8,128)(4,1)S(1)}, pred[2,8,16,256]{3,2,1,0:T(8,128)(4,1)}, u32[]{:S(2)}) copy-start(pred[2,8,16,256]{3,2,1,0:T(8,128)(4,1)} %get-tuple-element.19) | copy-start | bytes 196612
  203.9 3.1 %copy-start.18 = (pred[2,8,16,256]{3,2,1,0:T(8,128)(4,1)S(1)}, pred[2,8,16,256]{3,2,1,0:T(8,128)(4,1)}, u32[]{:S(2)}) copy-start(pred[2,8,16,256]{3,2,1,0:T(8,128)(4,1)} %get-tuple-element.20) | copy-start | bytes 196612
  203.9 3.1 %copy-start.19 = (pred[2,8,16,256]{3,2,1,0:T(8,128)(4,1)S(1)}, pred[2,8,16,256]{3,2,1,0:T(8,128)(4,1)}, u32[]{:S(2)}) copy-start(pred[2,8,16,256]{3,2,1,0:T(8,128)(4,1)} %get-tuple-element.21) | copy-start | bytes 196612
  203.9 3.1 %copy-start.20 = (pred[2,8,16,256]{3,2,1,0:T(8,128)(4,1)S(1)}, pred[2,8,16,256]{3,2,1,0:T(8,128)(4,1)}, u32[]{:S(2)}) copy-start(pred[2,8,16,256]{3,2,1,0:T(8,128)(4,1)} %get-tuple-element.22) | copy-start | bytes 196612
  206.9 6.3 %copy-start.1 = (f32[2,2,8,16,256]{4,3,2,1,0:T(8,128)S(1)}, f32[2,2,8,16,256]{4,3,2,1,0:T(8,128)}, u32[]{:S(2)}) copy-start(f32[2,2,8,16,256]{4,3,2,1,0:T(8,128)} %get-tuple-element.24) | copy-start | bytes 1572868
  207.0 6.3 %copy-start.2 = (f32[2,8,16,256]{3,2,1,0:T(8,128)S(1)}, f32[2,8,16,256]{3,2,1,0:T(8,128)}, u32[]{:S(2)}) copy-start(f32[2,8,16,256]{3,2,1,0:T(8,128)} %fusion.28) | copy-start | bytes 786436
  (2 other events, 3.9 us)
where the time goes:
time: 215 us
  blocking collectives  161 us (75%)
  other arithmetic  29.3 us (14%)
  starting transfers between devices  10.1 us (5%)
  local copies, waits for them, and re-layouts  7.45 us (3%)
  matrix products  3.4 us (2%)
    unnamed x2, blocking collectives  126 us
    all_gather x2, blocking collectives, per_device(): lax.all_gather(traction_spectrum, 'long', axis=0, tiled=True)  35 us
    ppermute x2, starting transfers between devices, padded_2(): lax.ppermute(lax.slice_in_dim(block, 0, width, axis=dim), axis, backward)  9.16 us
    sub x1, other arithmetic, advance(): 1.0 - (1.0 - dmg_mid) * jnp.exp(-rate_mid * jax.nn.softplus(energy - limi...  6.16 us
    sub x1, other arithmetic, per_device(): stiffness = 1.0 - damage  6.15 us
  transfers between devices with their start and end apart: 4, of which 1 were waited for; matrix products, arithmetic and copies ran while one was open for 1% of the time, Pallas kernels for 0%

commit v1 on v0

--- a/solution.py
+++ b/solution.py
@@ -6,6 +6,28 @@
 
 STEPS = 2
 time_step = 0.5
+
+
+def joined_along(parts, dim):
+    parts = jnp.moveaxis(parts, 0, dim)
+    dims = parts.shape
+    return parts.reshape(*dims[:dim], dims[dim] * dims[dim + 1], *dims[dim + 2 :])
+
+
+def collect(array, axis, dim):
+    size = lax.axis_size(axis)
+    pairs = [(i, (i + 1) % size) for i in range(size)]
+    back = [(b, a) for a, b in pairs]
+    lower, upper = ([], [])
+    for step in range(size - 1):
+        if step % 2 == 0:
+            lower.append(lax.ppermute(lower[-1] if lower else array, axis, pairs))
+        else:
+            upper.append(lax.ppermute(upper[-1] if upper else array, axis, back))
+    tiles = jnp.stack([*lower[::-1], array, *upper])
+    shift = lax.axis_index(axis) - len(lower)
+    tiles = tiles[(jnp.arange(size) - shift) % size]
+    return joined_along(tiles, dim)
 
 
 def padded_2(block, sides, width):
@@ -148,7 +170,7 @@
             places = position * cells + jnp.arange(cells, dtype=jnp.int32)
             return wave_sum(waves, places, piece, length, norming)
 
-        traction = add_waves(lax.all_gather(traction_spectrum, "long", axis=0, tiled=True))
+        traction = add_waves(collect(traction_spectrum, "long", 0))
         displacement, velocity, damage = advance(
             displacement, velocity, damage, rates, limits, on_fault, forces, energy, traction, signs
         )

time: 215 us -> 273 us (1.27)
  starting transfers between devices: 10.1 us -> 72.4 us
  blocking collectives: 161 us -> 125 us
  waiting for transfers between devices: 1.76 us -> 20.9 us
  local copies, waits for them, and re-layouts: 7.45 us -> 17.4 us
  other arithmetic: 29.3 us -> 33.1 us
    ppermute x0 -> x30, starting transfers between devices: none -> 62.3 us  [the longest x14 62.1 us: collect(): upper.append(lax.ppermute(upper[-1] if upper else array, axis, back))]
    all_gather x2 -> x0, blocking collectives: 35 us -> none  [per_device(): lax.all_gather(traction_spectrum, 'long', axis=0, tiled=True)]
    ppermute x0 -> x30, waiting for transfers between devices: none -> 18.6 us  [the longest x16 13.8 us: collect(): lower.append(lax.ppermute(lower[-1] if lower else array, axis, pairs))]
    unnamed x63 -> x57, local copies, waits for them, and re-layouts: 1.91 us -> 9.15 us
    gather x0 -> x4, local copies, waits for them, and re-layouts: none -> 4.13 us  [collect(): tiles = tiles[(jnp.arange(size) - shift) % size]]
  transfers between devices with their start and end apart: 4 -> 34, of which waited for: 1 -> 16; matrix products, arithmetic and copies ran while one was open for 1% -> 11% of each run, Pallas kernels for 0% -> 0%
where the time goes in v1:
time: 273 us
  blocking collectives  125 us (46%)
  starting transfers between devices  72.4 us (27%)
  other arithmetic  33.1 us (12%)
  waiting for transfers between devices  20.9 us (8%)
  local copies, waits for them, and re-layouts  17.4 us (6%)
    unnamed x2, blocking collectives  125 us
    ppermute x14, starting transfers between devices, collect(): upper.append(lax.ppermute(upper[-1] if upper else array, axis, back))  62.1 us
    ppermute x16, waiting for transfers between devices, collect(): lower.append(lax.ppermute(lower[-1] if lower else array, axis, pairs))  13.8 us
    ppermute x2, starting transfers between devices, padded_2(): lax.ppermute(lax.slice_in_dim(block, 0, width, axis=dim), axis, backward)  9.52 us
    unnamed x57, local copies, waits for them, and re-layouts  9.15 us
    sub x1, other arithmetic, per_device(): stiffness = 1.0 - damage  7.19 us
    sub x1, other arithmetic, advance(): 1.0 - (1.0 - dmg_mid) * jnp.exp(-rate_mid * jax.nn.softplus(energy - limi...  6.1 us
    add x2, other arithmetic, advance(): disp_new = disp_mid + time_step * vel_new  5.86 us
  transfers between devices with their start and end apart: 34, of which 16 were waited for; matrix products, arithmetic and copies ran while one was open for 11% of the time, Pallas kernels for 0%

profile of v1, /device:TPU:0, one launch (start us, length us, event | category | flops | bytes accessed | tf_op | source)
XLA Modules:
  0.0 272.6 jit_solution(18168414912511501956)
XLA Ops:
  3.1 5.1 %collective-permute-start.1 = (f32[3,2,1,16,256]{4,3,2,1,0:T(8,128)S(1)}, f32[3,2,1,16,256]{4,3,2,1,0:T(8,128)S(1)}, u32[]{:S(2)}, u32[]{:S(2)}) collective-permute-start(f32[3,2,1,16,256]{4,3,2,1,0:T(8,128)S(1)} %get-tuple-element.28), channel_id=1, source_target_pairs={{1,0},{2,1},{3,2},{4,3},{5,4},{6,5},{7,6},{8,7},{9,8},{10,9},{11,1... | collective-permute-start | bytes 294920 | tf_op jit(solution)/shard_map/ppermute | solution.py:42
  12.2 1.3 multiply_reduce_fusion.5
  15.5 62.1 %all-reduce.2 = f32[64,2,2,16]{3,2,1,0:T(2,128)} all-reduce(f32[64,2,2,16]{3,2,1,0:T(2,128)S(1)} %copy.45), channel_id=2, replica_groups=mesh['groups'=2,'long'=16] {'long'}, use_global_device_ids=true, to_apply=%region_1.2.clone | all-reduce | flops 4096 | bytes 32768
  79.4 4.4 %collective-permute-start.10 = (f32[4,2,2,16]{3,2,0,1:T(2,128)S(1)}, f32[4,2,2,16]{3,2,0,1:T(2,128)S(1)}, u32[]{:S(2)}, u32[]{:S(2)}) collective-permute-start(f32[4,2,2,16]{3,2,0,1:T(2,128)S(1)} %pad_maximum_fusion.35), channel_id=1, source_target_pairs={{1,0},{2,1},{3,2},{4,3},{5,4},{6,5},{7,6},{8,7},{9,8},{10,9},{11,1... | collective-permute-start | bytes 3080 | tf_op jit(solution)/shard_map/ppermute | solution.py:26
  83.9 1.3 collective-permute-done.2
  85.2 7.2 %fusion.15 = (f32[2,8,16,256]{3,2,1,0:T(8,128)S(1)}, pred[2,8,16,256]{3,2,1,0:T(8,128)(4,1)}, pred[2,8,16,256]{3,2,1,0:T(8,128)(4,1)}, pred[2,8,16,256]{3,2,1,0:T(8,128)(4,1)}, pred[2,8,16,256]{3,2,1,0:T(8,128)(4,1)}) fusion(f32[2,8,16,256]{3,2,1,0:T(8,128)S(1)} %get-tuple-element.7, f32[2,8,16,256]{3,2,1,0:T(8,128)} %get-tuple-element.58, ...), kind=kLoop, calls=%fused_computation.59 | loop fusion | flops 2162688 | bytes 1835040 | tf_op jit(solution)/shard_map/sub | solution.py:148
  92.4 4.5 %collective-permute-start.11 = (f32[4,2,2,16]{3,2,0,1:T(2,128)S(1)}, f32[4,2,2,16]{3,2,0,1:T(2,128)S(1)}, u32[]{:S(2)}, u32[]{:S(2)}) collective-permute-start(f32[4,2,2,16]{3,2,0,1:T(2,128)S(1)} %collective-permute-done.10), channel_id=1, source_target_pairs={{1,0},{2,1},{3,2},{4,3},{5,4},{6,5},{7,6},{8,7},{9,8},{10,9},{11,1... | collective-permute-start | bytes 3080 | tf_op jit(solution)/shard_map/ppermute | solution.py:26
  96.9 1.2 collective-permute-done.4
  98.3 4.4 %collective-permute-start.12 = (f32[4,2,2,16]{3,2,0,1:T(2,128)S(1)}, f32[4,2,2,16]{3,2,0,1:T(2,128)S(1)}, u32[]{:S(2)}, u32[]{:S(2)}) collective-permute-start(f32[4,2,2,16]{3,2,0,1:T(2,128)S(1)} %collective-permute-done.11), channel_id=1, source_target_pairs={{1,0},{2,1},{3,2},{4,3},{5,4},{6,5},{7,6},{8,7},{9,8},{10,9},{11,1... | collective-permute-start | bytes 3080 | tf_op jit(solution)/shard_map/ppermute | solution.py:26
  102.7 1.2 collective-permute-done.5
  104.1 4.4 %collective-permute-start.13 = (f32[4,2,2,16]{3,2,0,1:T(2,128)S(1)}, f32[4,2,2,16]{3,2,0,1:T(2,128)S(1)}, u32[]{:S(2)}, u32[]{:S(2)}) collective-permute-start(f32[4,2,2,16]{3,2,0,1:T(2,128)S(1)} %collective-permute-done.12), channel_id=1, source_target_pairs={{1,0},{2,1},{3,2},{4,3},{5,4},{6,5},{7,6},{8,7},{9,8},{10,9},{11,1... | collective-permute-start | bytes 3080 | tf_op jit(solution)/shard_map/ppermute | solution.py:26
  109.9 4.5 %collective-permute-start.14 = (f32[4,2,2,16]{3,2,0,1:T(2,128)S(1)}, f32[4,2,2,16]{3,2,0,1:T(2,128)S(1)}, u32[]{:S(2)}, u32[]{:S(2)}) collective-permute-start(f32[4,2,2,16]{3,2,0,1:T(2,128)S(1)} %collective-permute-done.13), channel_id=1, source_target_pairs={{1,0},{2,1},{3,2},{4,3},{5,4},{6,5},{7,6},{8,7},{9,8},{10,9},{11,1... | collective-permute-start | bytes 3080 | tf_op jit(solution)/shard_map/ppermute | solution.py:26
  115.5 1.3 fusion.33
  116.8 4.4 %collective-permute-start.15 = (f32[4,2,2,16]{3,2,0,1:T(2,128)S(1)}, f32[4,2,2,16]{3,2,0,1:T(2,128)S(1)}, u32[]{:S(2)}, u32[]{:S(2)}) collective-permute-start(f32[4,2,2,16]{3,2,0,1:T(2,128)S(1)} %collective-permute-done.14), channel_id=1, source_target_pairs={{1,0},{2,1},{3,2},{4,3},{5,4},{6,5},{7,6},{8,7},{9,8},{10,9},{11,1... | collective-permute-start | bytes 3080 | tf_op jit(solution)/shard_map/ppermute | solution.py:26
  122.6 4.4 %collective-permute-start.16 = (f32[4,2,2,16]{3,2,0,1:T(2,128)S(1)}, f32[4,2,2,16]{3,2,0,1:T(2,128)S(1)}, u32[]{:S(2)}, u32[]{:S(2)}) collective-permute-start(f32[4,2,2,16]{3,2,0,1:T(2,128)S(1)} %collective-permute-done.15), channel_id=1, source_target_pairs={{1,0},{2,1},{3,2},{4,3},{5,4},{6,5},{7,6},{8,7},{9,8},{10,9},{11,1... | collective-permute-start | bytes 3080 | tf_op jit(solution)/shard_map/ppermute | solution.py:26
  129.9 3.0 %multiply_add_fusion.2 = (f32[2,2,8,16,256]{4,3,2,1,0:T(8,128)S(1)}, f32[2,2,8,16,256]{4,3,2,1,0:T(8,128)}) fusion(f32[2,2,8,16,256]{4,3,2,1,0:T(8,128)S(1)} %copy-done, f32[2,2,8,16,256]{4,3,2,1,0:T(8,128)} %param.10, f32[2,8,16,256]{3,2,1,0:T(8,128)S(1)} %fusion.40, f32[2,2,8,16]{3,2,1,0:T(8,128)S(1)} %broadcast_multiply_fusion.1, ...), kind=kLoop, calls=%fused_computation.48 | loop fusion | flops 3538944 | bytes 6490112 | tf_op jit(solution)/shard_map/add | solution.py:130
  132.9 4.5 %collective-permute-start.18 = (f32[3,2,1,16,256]{4,3,2,1,0:T(8,128)S(1)}, f32[3,2,1,16,256]{4,3,2,1,0:T(8,128)S(1)}, u32[]{:S(2)}, u32[]{:S(2)}) collective-permute-start(f32[3,2,1,16,256]{4,3,2,1,0:T(8,128)S(1)} %get-tuple-element.26), channel_id=1, source_target_pairs={{1,0},{2,1},{3,2},{4,3},{5,4},{6,5},{7,6},{8,7},{9,8},{10,9},{11,1... | collective-permute-start | bytes 294920 | tf_op jit(solution)/shard_map/ppermute | solution.py:42
  137.4 2.3 collective-permute-done.17
  141.2 62.8 %all-reduce.3 = f32[64,2,2,16]{3,2,1,0:T(2,128)S(1)} all-reduce(f32[64,2,2,16]{3,2,1,0:T(2,128)S(1)} %copy.52), channel_id=3, replica_groups=mesh['groups'=2,'long'=16] {'long'}, use_global_device_ids=true, to_apply=%region_8.9.clone | all-reduce | flops 4096 | bytes 32768
  204.4 4.4 %collective-permute-start.27 = (f32[4,2,2,16]{3,2,0,1:T(2,128)S(1)}, f32[4,2,2,16]{3,2,0,1:T(2,128)S(1)}, u32[]{:S(2)}, u32[]{:S(2)}) collective-permute-start(f32[4,2,2,16]{3,2,0,1:T(2,128)S(1)} %pad_maximum_fusion.36), channel_id=1, source_target_pairs={{1,0},{2,1},{3,2},{4,3},{5,4},{6,5},{7,6},{8,7},{9,8},{10,9},{11,1... | collective-permute-start | bytes 3080 | tf_op jit(solution)/shard_map/ppermute | solution.py:26
  210.2 5.7 %collective-permute-done.20 = f32[4,2,2,16]{3,2,0,1:T(2,128)S(1)} collective-permute-done((f32[4,2,2,16]{3,2,0,1:T(2,128)S(1)}, f32[4,2,2,16]{3,2,0,1:T(2,128)S(1)}, u32[]{:S(2)}, u32[]{:S(2)}) %collective-permute-start.20) | collective-permute-done | bytes 1056 | tf_op jit(solution)/shard_map/ppermute | solution.py:24
  216.1 4.5 %collective-permute-start.28 = (f32[4,2,2,16]{3,2,0,1:T(2,128)S(1)}, f32[4,2,2,16]{3,2,0,1:T(2,128)S(1)}, u32[]{:S(2)}, u32[]{:S(2)}) collective-permute-start(f32[4,2,2,16]{3,2,0,1:T(2,128)S(1)} %collective-permute-done.27), channel_id=1, source_target_pairs={{1,0},{2,1},{3,2},{4,3},{5,4},{6,5},{7,6},{8,7},{9,8},{10,9},{11,1... | collective-permute-start | bytes 3080 | tf_op jit(solution)/shard_map/ppermute | solution.py:26
  221.7 1.4 fusion.23
  223.1 4.5 %collective-permute-start.29 = (f32[4,2,2,16]{3,2,0,1:T(2,128)S(1)}, f32[4,2,2,16]{3,2,0,1:T(2,128)S(1)}, u32[]{:S(2)}, u32[]{:S(2)}) collective-permute-start(f32[4,2,2,16]{3,2,0,1:T(2,128)S(1)} %collective-permute-done.28), channel_id=1, source_target_pairs={{1,0},{2,1},{3,2},{4,3},{5,4},{6,5},{7,6},{8,7},{9,8},{10,9},{11,1... | collective-permute-start | bytes 3080 | tf_op jit(solution)/shard_map/ppermute | solution.py:26
  229.0 4.4 %collective-permute-start.30 = (f32[4,2,2,16]{3,2,0,1:T(2,128)S(1)}, f32[4,2,2,16]{3,2,0,1:T(2,128)S(1)}, u32[]{:S(2)}, u32[]{:S(2)}) collective-permute-start(f32[4,2,2,16]{3,2,0,1:T(2,128)S(1)} %collective-permute-done.29), channel_id=1, source_target_pairs={{1,0},{2,1},{3,2},{4,3},{5,4},{6,5},{7,6},{8,7},{9,8},{10,9},{11,1... | collective-permute-start | bytes 3080 | tf_op jit(solution)/shard_map/ppermute | solution.py:26
  233.4 6.1 %fusion.19 = f32[2,8,16,256]{3,2,1,0:T(8,128)} fusion(f32[2,8,16,256]{3,2,1,0:T(8,128)S(1)} %get-tuple-element.18, f32[2,8,16,256]{3,2,1,0:T(8,128)S(1)} %get-tuple-element.5, f32[2,8,16,256]{3,2,1,0:T(8,128)S(1)} %copy-done.2, f32[2,8,16,256]{3,2,1,0:T(8,128)S(1)} %get-tuple-element.4, pred[2,8,16,256]{3,2,1,0:T(8,128)(4,1)S(1)} %copy-done.8, ...), kind=kLoop, calls=%fused_computation.63 | loop fusion | flops 1769472 | bytes 1572896 | tf_op jit(solution)/shard_map/sub | solution.py:131
  239.6 4.4 %collective-permute-start.31 = (f32[4,2,2,16]{3,2,0,1:T(2,128)S(1)}, f32[4,2,2,16]{3,2,0,1:T(2,128)S(1)}, u32[]{:S(2)}, u32[]{:S(2)}) collective-permute-start(f32[4,2,2,16]{3,2,0,1:T(2,128)S(1)} %collective-permute-done.30), channel_id=1, source_target_pairs={{1,0},{2,1},{3,2},{4,3},{5,4},{6,5},{7,6},{8,7},{9,8},{10,9},{11,1... | collective-permute-start | bytes 3080 | tf_op jit(solution)/shard_map/ppermute | solution.py:26
  244.0 1.3 collective-permute-done.31
  245.3 4.4 %collective-permute-start.32 = (f32[4,2,2,16]{3,2,0,1:T(2,128)S(1)}, f32[4,2,2,16]{3,2,0,1:T(2,128)S(1)}, u32[]{:S(2)}, u32[]{:S(2)}) collective-permute-start(f32[4,2,2,16]{3,2,0,1:T(2,128)S(1)} %collective-permute-done.31), channel_id=1, source_target_pairs={{1,0},{2,1},{3,2},{4,3},{5,4},{6,5},{7,6},{8,7},{9,8},{10,9},{11,1... | collective-permute-start | bytes 3080 | tf_op jit(solution)/shard_map/ppermute | solution.py:26
  251.1 4.4 %collective-permute-start.33 = (f32[4,2,2,16]{3,2,0,1:T(2,128)S(1)}, f32[4,2,2,16]{3,2,0,1:T(2,128)S(1)}, u32[]{:S(2)}, u32[]{:S(2)}) collective-permute-start(f32[4,2,2,16]{3,2,0,1:T(2,128)S(1)} %collective-permute-done.32), channel_id=1, source_target_pairs={{1,0},{2,1},{3,2},{4,3},{5,4},{6,5},{7,6},{8,7},{9,8},{10,9},{11,1... | collective-permute-start | bytes 3080 | tf_op jit(solution)/shard_map/ppermute | solution.py:26
  265.1 2.3 gather_fusion.1
  269.7 2.9 %multiply_add_fusion = (f32[2,2,8,16,256]{4,3,2,1,0:T(8,128)}, f32[2,2,8,16,256]{4,3,2,1,0:T(8,128)}) fusion(f32[2,2,8,16,256]{4,3,2,1,0:T(8,128)S(1)} %get-tuple-element.23, f32[2,2,8,16,256]{4,3,2,1,0:T(8,128)S(1)} %copy-done.1, f32[2,8,16,256]{3,2,1,0:T(8,128)S(1)} %fusion.40, f32[2,2,8,16]{3,2,1,0:T(8,128)S(1)} %broadcast_multiply_fusion, ...), kind=kLoop, calls=%fused_computation.42 | loop fusion | flops 3538944 | bytes 6490112 | tf_op jit(solution)/shard_map/add | solution.py:130
  (162 shorter events, 35.6 us)
Async XLA Ops:
  2.6 9.1 %collective-permute-start = (f32[3,2,1,16,256]{4,3,2,1,0:T(8,128)S(1)}, f32[3,2,1,16,256]{4,3,2,1,0:T(8,128)S(1)}, u32[]{:S(2)}, u32[]{:S(2)}) collective-permute-start(f32[3,2,1,16,256]{4,3,2,1,0:T(8,128)S(1)} %get-tuple-element.27), channel_id=1, source_target_pairs={{0,1},{1,2},{2,3},{3,4},{4,5},{5,6},{6,7},{7,8},{8,9},{9,10},{10,1... | collective-permute-start | bytes 294920 | tf_op jit(solution)/shard_map/ppermute | solution.py:39
  3.1 8.6 %collective-permute-start.1 = (f32[3,2,1,16,256]{4,3,2,1,0:T(8,128)S(1)}, f32[3,2,1,16,256]{4,3,2,1,0:T(8,128)S(1)}, u32[]{:S(2)}, u32[]{:S(2)}) collective-permute-start(f32[3,2,1,16,256]{4,3,2,1,0:T(8,128)S(1)} %get-tuple-element.28), channel_id=1, source_target_pairs={{1,0},{2,1},{3,2},{4,3},{5,4},{6,5},{7,6},{8,7},{9,8},{10,9},{11,1... | collective-permute-start | bytes 294920 | tf_op jit(solution)/shard_map/ppermute | solution.py:42
  79.4 5.8 %collective-permute-start.2 = (f32[4,2,2,16]{3,2,0,1:T(2,128)S(1)}, f32[4,2,2,16]{3,2,0,1:T(2,128)S(1)}, u32[]{:S(2)}, u32[]{:S(2)}) collective-permute-start(f32[4,2,2,16]{3,2,0,1:T(2,128)S(1)} %pad_maximum_fusion.35), channel_id=1, source_target_pairs={{0,1},{1,2},{2,3},{3,4},{4,5},{5,6},{6,7},{7,8},{8,9},{9,10},{10,1... | collective-permute-start | bytes 3080 | tf_op jit(solution)/shard_map/ppermute | solution.py:24
  79.4 13.0 %collective-permute-start.10 = (f32[4,2,2,16]{3,2,0,1:T(2,128)S(1)}, f32[4,2,2,16]{3,2,0,1:T(2,128)S(1)}, u32[]{:S(2)}, u32[]{:S(2)}) collective-permute-start(f32[4,2,2,16]{3,2,0,1:T(2,128)S(1)} %pad_maximum_fusion.35), channel_id=1, source_target_pairs={{1,0},{2,1},{3,2},{4,3},{5,4},{6,5},{7,6},{8,7},{9,8},{10,9},{11,1... | collective-permute-start | bytes 3080 | tf_op jit(solution)/shard_map/ppermute | solution.py:26
  85.2 7.2 %collective-permute-start.3 = (f32[4,2,2,16]{3,2,0,1:T(2,128)S(1)}, f32[4,2,2,16]{3,2,0,1:T(2,128)S(1)}, u32[]{:S(2)}, u32[]{:S(2)}) collective-permute-start(f32[4,2,2,16]{3,2,0,1:T(2,128)S(1)} %collective-permute-done.2), channel_id=1, source_target_pairs={{0,1},{1,2},{2,3},{3,4},{4,5},{5,6},{6,7},{7,8},{8,9},{9,10},{10,1... | collective-permute-start | bytes 3080 | tf_op jit(solution)/shard_map/ppermute | solution.py:24
  92.4 5.8 %collective-permute-start.4 = (f32[4,2,2,16]{3,2,0,1:T(2,128)S(1)}, f32[4,2,2,16]{3,2,0,1:T(2,128)S(1)}, u32[]{:S(2)}, u32[]{:S(2)}) collective-permute-start(f32[4,2,2,16]{3,2,0,1:T(2,128)S(1)} %collective-permute-done.3), channel_id=1, source_target_pairs={{0,1},{1,2},{2,3},{3,4},{4,5},{5,6},{6,7},{7,8},{8,9},{9,10},{10,1... | collective-permute-start | bytes 3080 | tf_op jit(solution)/shard_map/ppermute | solution.py:24
  92.4 5.9 %collective-permute-start.11 = (f32[4,2,2,16]{3,2,0,1:T(2,128)S(1)}, f32[4,2,2,16]{3,2,0,1:T(2,128)S(1)}, u32[]{:S(2)}, u32[]{:S(2)}) collective-permute-start(f32[4,2,2,16]{3,2,0,1:T(2,128)S(1)} %collective-permute-done.10), channel_id=1, source_target_pairs={{1,0},{2,1},{3,2},{4,3},{5,4},{6,5},{7,6},{8,7},{9,8},{10,9},{11,1... | collective-permute-start | bytes 3080 | tf_op jit(solution)/shard_map/ppermute | solution.py:26
  98.3 5.8 %collective-permute-start.12 = (f32[4,2,2,16]{3,2,0,1:T(2,128)S(1)}, f32[4,2,2,16]{3,2,0,1:T(2,128)S(1)}, u32[]{:S(2)}, u32[]{:S(2)}) collective-permute-start(f32[4,2,2,16]{3,2,0,1:T(2,128)S(1)} %collective-permute-done.11), channel_id=1, source_target_pairs={{1,0},{2,1},{3,2},{4,3},{5,4},{6,5},{7,6},{8,7},{9,8},{10,9},{11,1... | collective-permute-start | bytes 3080 | tf_op jit(solution)/shard_map/ppermute | solution.py:26
  103.9 5.8 %collective-permute-start.6 = (f32[4,2,2,16]{3,2,0,1:T(2,128)S(1)}, f32[4,2,2,16]{3,2,0,1:T(2,128)S(1)}, u32[]{:S(2)}, u32[]{:S(2)}) collective-permute-start(f32[4,2,2,16]{3,2,0,1:T(2,128)S(1)} %collective-permute-done.5), channel_id=1, source_target_pairs={{0,1},{1,2},{2,3},{3,4},{4,5},{5,6},{6,7},{7,8},{8,9},{9,10},{10,1... | collective-permute-start | bytes 3080 | tf_op jit(solution)/shard_map/ppermute | solution.py:24
  104.1 5.8 %collective-permute-start.13 = (f32[4,2,2,16]{3,2,0,1:T(2,128)S(1)}, f32[4,2,2,16]{3,2,0,1:T(2,128)S(1)}, u32[]{:S(2)}, u32[]{:S(2)}) collective-permute-start(f32[4,2,2,16]{3,2,0,1:T(2,128)S(1)} %collective-permute-done.12), channel_id=1, source_target_pairs={{1,0},{2,1},{3,2},{4,3},{5,4},{6,5},{7,6},{8,7},{9,8},{10,9},{11,1... | collective-permute-start | bytes 3080 | tf_op jit(solution)/shard_map/ppermute | solution.py:26
  109.7 5.8 %collective-permute-start.7 = (f32[4,2,2,16]{3,2,0,1:T(2,128)S(1)}, f32[4,2,2,16]{3,2,0,1:T(2,128)S(1)}, u32[]{:S(2)}, u32[]{:S(2)}) collective-permute-start(f32[4,2,2,16]{3,2,0,1:T(2,128)S(1)} %collective-permute-done.6), channel_id=1, source_target_pairs={{0,1},{1,2},{2,3},{3,4},{4,5},{5,6},{6,7},{7,8},{8,9},{9,10},{10,1... | collective-permute-start | bytes 3080 | tf_op jit(solution)/shard_map/ppermute | solution.py:24
  109.9 6.9 %collective-permute-start.14 = (f32[4,2,2,16]{3,2,0,1:T(2,128)S(1)}, f32[4,2,2,16]{3,2,0,1:T(2,128)S(1)}, u32[]{:S(2)}, u32[]{:S(2)}) collective-permute-start(f32[4,2,2,16]{3,2,0,1:T(2,128)S(1)} %collective-permute-done.13), channel_id=1, source_target_pairs={{1,0},{2,1},{3,2},{4,3},{5,4},{6,5},{7,6},{8,7},{9,8},{10,9},{11,1... | collective-permute-start | bytes 3080 | tf_op jit(solution)/shard_map/ppermute | solution.py:26
  115.5 5.8 %collective-permute-start.8 = (f32[4,2,2,16]{3,2,0,1:T(2,128)S(1)}, f32[4,2,2,16]{3,2,0,1:T(2,128)S(1)}, u32[]{:S(2)}, u32[]{:S(2)}) collective-permute-start(f32[4,2,2,16]{3,2,0,1:T(2,128)S(1)} %collective-permute-done.7), channel_id=1, source_target_pairs={{0,1},{1,2},{2,3},{3,4},{4,5},{5,6},{6,7},{7,8},{8,9},{9,10},{10,1... | collective-permute-start | bytes 3080 | tf_op jit(solution)/shard_map/ppermute | solution.py:24
  116.8 5.8 %collective-permute-start.15 = (f32[4,2,2,16]{3,2,0,1:T(2,128)S(1)}, f32[4,2,2,16]{3,2,0,1:T(2,128)S(1)}, u32[]{:S(2)}, u32[]{:S(2)}) collective-permute-start(f32[4,2,2,16]{3,2,0,1:T(2,128)S(1)} %collective-permute-done.14), channel_id=1, source_target_pairs={{1,0},{2,1},{3,2},{4,3},{5,4},{6,5},{7,6},{8,7},{9,8},{10,9},{11,1... | collective-permute-start | bytes 3080 | tf_op jit(solution)/shard_map/ppermute | solution.py:26
  121.3 5.8 %collective-permute-start.9 = (f32[4,2,2,16]{3,2,0,1:T(2,128)S(1)}, f32[4,2,2,16]{3,2,0,1:T(2,128)S(1)}, u32[]{:S(2)}, u32[]{:S(2)}) collective-permute-start(f32[4,2,2,16]{3,2,0,1:T(2,128)S(1)} %collective-permute-done.8), channel_id=1, source_target_pairs={{0,1},{1,2},{2,3},{3,4},{4,5},{5,6},{6,7},{7,8},{8,9},{9,10},{10,1... | collective-permute-start | bytes 3080 | tf_op jit(solution)/shard_map/ppermute | solution.py:24
  122.6 5.8 %collective-permute-start.16 = (f32[4,2,2,16]{3,2,0,1:T(2,128)S(1)}, f32[4,2,2,16]{3,2,0,1:T(2,128)S(1)}, u32[]{:S(2)}, u32[]{:S(2)}) collective-permute-start(f32[4,2,2,16]{3,2,0,1:T(2,128)S(1)} %collective-permute-done.15), channel_id=1, source_target_pairs={{1,0},{2,1},{3,2},{4,3},{5,4},{6,5},{7,6},{8,7},{9,8},{10,9},{11,1... | collective-permute-start | bytes 3080 | tf_op jit(solution)/shard_map/ppermute | solution.py:26
  132.8 6.8 %collective-permute-start.17 = (f32[3,2,1,16,256]{4,3,2,1,0:T(8,128)S(1)}, f32[3,2,1,16,256]{4,3,2,1,0:T(8,128)S(1)}, u32[]{:S(2)}, u32[]{:S(2)}) collective-permute-start(f32[3,2,1,16,256]{4,3,2,1,0:T(8,128)S(1)} %get-tuple-element.25), channel_id=1, source_target_pairs={{0,1},{1,2},{2,3},{3,4},{4,5},{5,6},{6,7},{7,8},{8,9},{9,10},{10,1... | collective-permute-start | bytes 294920 | tf_op jit(solution)/shard_map/ppermute | solution.py:39
  132.9 6.7 %collective-permute-start.18 = (f32[3,2,1,16,256]{4,3,2,1,0:T(8,128)S(1)}, f32[3,2,1,16,256]{4,3,2,1,0:T(8,128)S(1)}, u32[]{:S(2)}, u32[]{:S(2)}) collective-permute-start(f32[3,2,1,16,256]{4,3,2,1,0:T(8,128)S(1)} %get-tuple-element.26), channel_id=1, source_target_pairs={{1,0},{2,1},{3,2},{4,3},{5,4},{6,5},{7,6},{8,7},{9,8},{10,9},{11,1... | collective-permute-start | bytes 294920 | tf_op jit(solution)/shard_map/ppermute | solution.py:42
  204.3 5.8 %collective-permute-start.19 = (f32[4,2,2,16]{3,2,0,1:T(2,128)S(1)}, f32[4,2,2,16]{3,2,0,1:T(2,128)S(1)}, u32[]{:S(2)}, u32[]{:S(2)}) collective-permute-start(f32[4,2,2,16]{3,2,0,1:T(2,128)S(1)} %pad_maximum_fusion.36), channel_id=1, source_target_pairs={{0,1},{1,2},{2,3},{3,4},{4,5},{5,6},{6,7},{7,8},{8,9},{9,10},{10,1... | collective-permute-start | bytes 3080 | tf_op jit(solution)/shard_map/ppermute | solution.py:24
  204.4 11.7 %collective-permute-start.27 = (f32[4,2,2,16]{3,2,0,1:T(2,128)S(1)}, f32[4,2,2,16]{3,2,0,1:T(2,128)S(1)}, u32[]{:S(2)}, u32[]{:S(2)}) collective-permute-start(f32[4,2,2,16]{3,2,0,1:T(2,128)S(1)} %pad_maximum_fusion.36), channel_id=1, source_target_pairs={{1,0},{2,1},{3,2},{4,3},{5,4},{6,5},{7,6},{8,7},{9,8},{10,9},{11,1... | collective-permute-start | bytes 3080 | tf_op jit(solution)/shard_map/ppermute | solution.py:26
  210.2 5.8 %collective-permute-start.20 = (f32[4,2,2,16]{3,2,0,1:T(2,128)S(1)}, f32[4,2,2,16]{3,2,0,1:T(2,128)S(1)}, u32[]{:S(2)}, u32[]{:S(2)}) collective-permute-start(f32[4,2,2,16]{3,2,0,1:T(2,128)S(1)} %collective-permute-done.19), channel_id=1, source_target_pairs={{0,1},{1,2},{2,3},{3,4},{4,5},{5,6},{6,7},{7,8},{8,9},{9,10},{10,1... | collective-permute-start | bytes 3080 | tf_op jit(solution)/shard_map/ppermute | solution.py:24
  215.9 5.8 %collective-permute-start.21 = (f32[4,2,2,16]{3,2,0,1:T(2,128)S(1)}, f32[4,2,2,16]{3,2,0,1:T(2,128)S(1)}, u32[]{:S(2)}, u32[]{:S(2)}) collective-permute-start(f32[4,2,2,16]{3,2,0,1:T(2,128)S(1)} %collective-permute-done.20), channel_id=1, source_target_pairs={{0,1},{1,2},{2,3},{3,4},{4,5},{5,6},{6,7},{7,8},{8,9},{9,10},{10,1... | collective-permute-start | bytes 3080 | tf_op jit(solution)/shard_map/ppermute | solution.py:24
  216.1 7.0 %collective-permute-start.28 = (f32[4,2,2,16]{3,2,0,1:T(2,128)S(1)}, f32[4,2,2,16]{3,2,0,1:T(2,128)S(1)}, u32[]{:S(2)}, u32[]{:S(2)}) collective-permute-start(f32[4,2,2,16]{3,2,0,1:T(2,128)S(1)} %collective-permute-done.27), channel_id=1, source_target_pairs={{1,0},{2,1},{3,2},{4,3},{5,4},{6,5},{7,6},{8,7},{9,8},{10,9},{11,1... | collective-permute-start | bytes 3080 | tf_op jit(solution)/shard_map/ppermute | solution.py:26
  221.7 5.9 %collective-permute-start.22 = (f32[4,2,2,16]{3,2,0,1:T(2,128)S(1)}, f32[4,2,2,16]{3,2,0,1:T(2,128)S(1)}, u32[]{:S(2)}, u32[]{:S(2)}) collective-permute-start(f32[4,2,2,16]{3,2,0,1:T(2,128)S(1)} %collective-permute-done.21), channel_id=1, source_target_pairs={{0,1},{1,2},{2,3},{3,4},{4,5},{5,6},{6,7},{7,8},{8,9},{9,10},{10,1... | collective-permute-start | bytes 3080 | tf_op jit(solution)/shard_map/ppermute | solution.py:24
  223.1 5.9 %collective-permute-start.29 = (f32[4,2,2,16]{3,2,0,1:T(2,128)S(1)}, f32[4,2,2,16]{3,2,0,1:T(2,128)S(1)}, u32[]{:S(2)}, u32[]{:S(2)}) collective-permute-start(f32[4,2,2,16]{3,2,0,1:T(2,128)S(1)} %collective-permute-done.28), channel_id=1, source_target_pairs={{1,0},{2,1},{3,2},{4,3},{5,4},{6,5},{7,6},{8,7},{9,8},{10,9},{11,1... | collective-permute-start | bytes 3080 | tf_op jit(solution)/shard_map/ppermute | solution.py:26
  227.6 5.8 %collective-permute-start.23 = (f32[4,2,2,16]{3,2,0,1:T(2,128)S(1)}, f32[4,2,2,16]{3,2,0,1:T(2,128)S(1)}, u32[]{:S(2)}, u32[]{:S(2)}) collective-permute-start(f32[4,2,2,16]{3,2,0,1:T(2,128)S(1)} %collective-permute-done.22), channel_id=1, source_target_pairs={{0,1},{1,2},{2,3},{3,4},{4,5},{5,6},{6,7},{7,8},{8,9},{9,10},{10,1... | collective-permute-start | bytes 3080 | tf_op jit(solution)/shard_map/ppermute | solution.py:24
  229.0 10.6 %collective-permute-start.30 = (f32[4,2,2,16]{3,2,0,1:T(2,128)S(1)}, f32[4,2,2,16]{3,2,0,1:T(2,128)S(1)}, u32[]{:S(2)}, u32[]{:S(2)}) collective-permute-start(f32[4,2,2,16]{3,2,0,1:T(2,128)S(1)} %collective-permute-done.29), channel_id=1, source_target_pairs={{1,0},{2,1},{3,2},{4,3},{5,4},{6,5},{7,6},{8,7},{9,8},{10,9},{11,1... | collective-permute-start | bytes 3080 | tf_op jit(solution)/shard_map/ppermute | solution.py:26
  233.4 10.6 %collective-permute-start.24 = (f32[4,2,2,16]{3,2,0,1:T(2,128)S(1)}, f32[4,2,2,16]{3,2,0,1:T(2,128)S(1)}, u32[]{:S(2)}, u32[]{:S(2)}) collective-permute-start(f32[4,2,2,16]{3,2,0,1:T(2,128)S(1)} %collective-permute-done.23), channel_id=1, source_target_pairs={{0,1},{1,2},{2,3},{3,4},{4,5},{5,6},{6,7},{7,8},{8,9},{9,10},{10,1... | collective-permute-start | bytes 3080 | tf_op jit(solution)/shard_map/ppermute | solution.py:24
  239.6 5.8 %collective-permute-start.31 = (f32[4,2,2,16]{3,2,0,1:T(2,128)S(1)}, f32[4,2,2,16]{3,2,0,1:T(2,128)S(1)}, u32[]{:S(2)}, u32[]{:S(2)}) collective-permute-start(f32[4,2,2,16]{3,2,0,1:T(2,128)S(1)} %collective-permute-done.30), channel_id=1, source_target_pairs={{1,0},{2,1},{3,2},{4,3},{5,4},{6,5},{7,6},{8,7},{9,8},{10,9},{11,1... | collective-permute-start | bytes 3080 | tf_op jit(solution)/shard_map/ppermute | solution.py:26
  244.0 5.8 %collective-permute-start.25 = (f32[4,2,2,16]{3,2,0,1:T(2,128)S(1)}, f32[4,2,2,16]{3,2,0,1:T(2,128)S(1)}, u32[]{:S(2)}, u32[]{:S(2)}) collective-permute-start(f32[4,2,2,16]{3,2,0,1:T(2,128)S(1)} %collective-permute-done.24), channel_id=1, source_target_pairs={{0,1},{1,2},{2,3},{3,4},{4,5},{5,6},{6,7},{7,8},{8,9},{9,10},{10,1... | collective-permute-start | bytes 3080 | tf_op jit(solution)/shard_map/ppermute | solution.py:24
  245.3 5.8 %collective-permute-start.32 = (f32[4,2,2,16]{3,2,0,1:T(2,128)S(1)}, f32[4,2,2,16]{3,2,0,1:T(2,128)S(1)}, u32[]{:S(2)}, u32[]{:S(2)}) collective-permute-start(f32[4,2,2,16]{3,2,0,1:T(2,128)S(1)} %collective-permute-done.31), channel_id=1, source_target_pairs={{1,0},{2,1},{3,2},{4,3},{5,4},{6,5},{7,6},{8,7},{9,8},{10,9},{11,1... | collective-permute-start | bytes 3080 | tf_op jit(solution)/shard_map/ppermute | solution.py:26
  251.1 13.4 %collective-permute-start.33 = (f32[4,2,2,16]{3,2,0,1:T(2,128)S(1)}, f32[4,2,2,16]{3,2,0,1:T(2,128)S(1)}, u32[]{:S(2)}, u32[]{:S(2)}) collective-permute-start(f32[4,2,2,16]{3,2,0,1:T(2,128)S(1)} %collective-permute-done.32), channel_id=1, source_target_pairs={{1,0},{2,1},{3,2},{4,3},{5,4},{6,5},{7,6},{8,7},{9,8},{10,9},{11,1... | collective-permute-start | bytes 3080 | tf_op jit(solution)/shard_map/ppermute | solution.py:26
  (18 other events, 387.6 us)
